TPU v7x, 32 devices: a whole 2x2x4 slice. The times are simulated.
32 devices in a mesh: scene: 2 (over y), seq: 4 (over z), head: 2 (over x), band: 2 (over core).
Axes of the slice: x: 2, y: 2, z: 4, core: 2. Of those that a mesh axis runs over, the one named last changes fastest.
Arguments:
- tokens: bfloat16 [8, 12, 37, 1024], P(('scene', 'seq'), ('head', 'band')), parts along dimension 0, may hold values from -6 to 6
- frame_gain: float32 [1024], replicated, may hold values from 0.5 to 1.5
- frame_qkv: bfloat16 [3, 1024, 1024], P(None, None, 'head'), may hold values from -6 to 6
- frame_out: bfloat16 [1024, 1024], P('head'), may hold values from -0.1875 to 0.1875
- global_gain: float32 [1024], replicated, may hold values from 0.5 to 1.5
- global_qkv: bfloat16 [3, 1024, 1024], P(None, None, 'head'), may hold values from -6 to 6
- global_out: bfloat16 [1024, 1024], P('head'), may hold values from -0.1875 to 0.1875
- head_gain: float32 [2048], replicated, may hold values from 0.5 to 1.5
- head_proj: bfloat16 [2048, 256], replicated, may hold values from -0.125 to 0.125
- head_bias: float32 [256], replicated, may hold values from -3 to 3
- head_conv: bfloat16 [3, 3, 256, 256], replicated, may hold values from -0.125 to 0.125
Outputs:
- blocks: bfloat16 [8, 12, 37, 1024], P(('scene', 'seq'), ('head', 'band')), parts along dimension 0
- features: bfloat16 [8, 12, 37, 256], P(('scene', 'seq'), ('head', 'band')), parts along dimension 0
There are 2 independent parts, one for each index of `scene`. A program takes and returns all parts, laid end to end along the dimension named above; an argument that names none is the same for every part. Nothing has to cross between parts.
All inputs are finite; a program needn't handle non-finite values.
Results may differ from a plain program's by a relative error of at most 0.017.
Values may be sent and summed in bfloat16 or wider, within the bound.
A program may use at most 256 MiB of HBM per device.

v0:
```python
import jax
import jax.numpy as jnp
from jax import lax
from jax.sharding import PartitionSpec as P

HD = 64
norm_eps = 1e-06
head_eps = 1e-05


def padded_2(block, sides, width):
    for axis, dim in sides:
        count = lax.axis_size(axis)
        forward = [(i, i + 1) for i in range(count - 1)]
        backward = [(target, source) for source, target in forward]
        low = lax.ppermute(
            lax.slice_in_dim(block, block.shape[dim] - width, None, axis=dim), axis, forward
        )
        high = lax.ppermute(lax.slice_in_dim(block, 0, width, axis=dim), axis, backward)
        block = jnp.concatenate([low, block, high], axis=dim)
    return block


def layer_norm(values, gain, epsilon):
    centre = values - jnp.mean(values, axis=-1, keepdims=True)
    spread = jnp.mean(centre * centre, axis=-1, keepdims=True)
    return centre * lax.rsqrt(spread + epsilon) * gain


def by_heads(matrix):
    return matrix.reshape(matrix.shape[0], matrix.shape[1] // HD, HD)


def attend_local(queries, keys_all, values_all):
    scores = jnp.einsum(
        "qhd,khd->qhk", by_heads(queries), by_heads(keys_all), preferred_element_type=jnp.float32
    ) * HD ** (-0.5)
    probs = jnp.exp(scores - jnp.max(scores, axis=-1, keepdims=True))
    mixed = jnp.einsum(
        "qhk,khd->qhd",
        probs.astype(jnp.bfloat16),
        by_heads(values_all),
        preferred_element_type=jnp.float32,
    )
    mixed = mixed / jnp.sum(probs, axis=-1)[..., None]
    return mixed.reshape(queries.shape).astype(jnp.bfloat16)


def key_step(local_rows, portion_rows):
    amount = portion_rows // local_rows
    best = 1
    for factor in range(1, amount + 1):
        if amount % factor == 0 and local_rows * factor <= max(local_rows, 1024):
            best = factor
    return local_rows * best


def fresh_carry(queries):
    heads_q = by_heads(queries)
    return (
        jnp.full(heads_q.shape[:2], -jnp.inf, jnp.float32),
        jnp.zeros(heads_q.shape[:2], jnp.float32),
        jnp.zeros(heads_q.shape, jnp.float32),
    )


def finish(carry, queries):
    return (carry[2] / carry[1][..., None]).reshape(queries.shape).astype(jnp.bfloat16)


def fold_keys(queries, carry, portions, local_rows):
    keys_in, values_in = portions
    step_rows = key_step(local_rows, keys_in.shape[0])
    heads_q = by_heads(queries)
    key_blocks = keys_in.reshape(-1, step_rows, keys_in.shape[1])
    value_blocks = values_in.reshape(-1, step_rows, values_in.shape[1])

    def absorb(states, blocks_pair):
        running_max, running_sum, weighted = states
        scores = jnp.einsum(
            "qhd,khd->qhk", heads_q, by_heads(blocks_pair[0]), preferred_element_type=jnp.float32
        ) * HD ** (-0.5)
        new_max = jnp.maximum(running_max, jnp.max(scores, axis=-1))
        decay = jnp.exp(running_max - new_max)
        probs = jnp.exp(scores - new_max[..., None])
        running_sum = running_sum * decay + jnp.sum(probs, axis=-1)
        weighted = weighted * decay[..., None] + jnp.einsum(
            "qhk,khd->qhd",
            probs.astype(jnp.bfloat16),
            by_heads(blocks_pair[1]),
            preferred_element_type=jnp.float32,
        )
        return ((new_max, running_sum, weighted), None)

    carry, ignored = lax.scan(absorb, carry, (key_blocks, value_blocks))
    return carry


def attention_block(inputs, gain, qkv_weight, out_weight, wide):
    normed = layer_norm(inputs.astype(jnp.float32), gain, norm_eps).astype(jnp.bfloat16)
    gathered = lax.all_gather(normed, "head", axis=1, tiled=True)
    flattened = gathered.reshape(-1, gathered.shape[-1])
    query_rows = jnp.dot(flattened, qkv_weight[0], preferred_element_type=jnp.float32).astype(
        jnp.bfloat16
    )
    key_rows = jnp.dot(flattened, qkv_weight[1], preferred_element_type=jnp.float32).astype(
        jnp.bfloat16
    )
    value_rows = jnp.dot(flattened, qkv_weight[2], preferred_element_type=jnp.float32).astype(
        jnp.bfloat16
    )
    if wide:
        carry = fold_keys(
            query_rows,
            fresh_carry(query_rows),
            (
                lax.all_gather(key_rows, ("seq", "band"), axis=0, tiled=True),
                lax.all_gather(value_rows, ("seq", "band"), axis=0, tiled=True),
            ),
            key_rows.shape[0],
        )
        attended = finish(carry, query_rows)
    else:
        keys_all, values_all = (
            lax.all_gather(key_rows, "band", axis=0, tiled=True),
            lax.all_gather(value_rows, "band", axis=0, tiled=True),
        )
        attended = attend_local(query_rows, keys_all, values_all)
    band_rows = inputs.shape[1] * inputs.shape[2]
    own_rows = lax.all_to_all(attended, "head", split_axis=0, concat_axis=1, tiled=True)
    branch = jnp.dot(
        own_rows,
        lax.all_gather(out_weight, "head", axis=0, tiled=True),
        preferred_element_type=jnp.float32,
    )
    merged = inputs.astype(jnp.float32).reshape(band_rows, -1) + branch
    return merged.astype(jnp.bfloat16).reshape(inputs.shape)


def on_device(
    tokens,
    frame_gain,
    frame_qkv,
    frame_out,
    global_gain,
    global_qkv,
    global_out,
    head_gain,
    head_proj,
    head_bias,
    head_conv,
):
    first = attention_block(tokens, frame_gain, frame_qkv, frame_out, False)
    second = attention_block(first, global_gain, global_qkv, global_out, True)
    band_height = tokens.shape[1]
    grid_width = tokens.shape[2]
    stacked = jnp.concatenate([first.astype(jnp.float32), second.astype(jnp.float32)], axis=-1)
    normed = layer_norm(stacked, head_gain, head_eps).astype(jnp.bfloat16)
    projected = (
        jnp.dot(
            normed.reshape(-1, stacked.shape[-1]), head_proj, preferred_element_type=jnp.float32
        )
        + head_bias
    )
    projected = projected.astype(jnp.bfloat16).reshape(
        tokens.shape[0], band_height, grid_width, head_proj.shape[1]
    )
    padded = padded_2(projected, ((("head", "band"), 1),), 1)
    padded = jnp.pad(padded, ((0, 0), (0, 0), (1, 1), (0, 0)))
    totals = jnp.zeros(projected.shape, jnp.float32)
    for offset_row in range(3):
        for offset_col in range(3):
            window = padded[
                :, offset_row : offset_row + band_height, offset_col : offset_col + grid_width
            ]
            totals = totals + jnp.einsum(
                "frcx,xy->frcy",
                window,
                head_conv[offset_row, offset_col],
                preferred_element_type=jnp.float32,
            )
    return (second, totals.astype(jnp.bfloat16))


def solution(mesh):
    return jax.shard_map(
        on_device,
        mesh=mesh,
        in_specs=(
            P(("scene", "seq"), ("head", "band"), None, None),
            P(),
            P(None, None, "head"),
            P("head", None),
            P(),
            P(None, None, "head"),
            P("head", None),
            P(),
            P(),
            P(),
            P(),
        ),
        out_specs=(
            P(("scene", "seq"), ("head", "band"), None, None),
            P(("scene", "seq"), ("head", "band"), None, None),
        ),
        check_vma=False,
    )
```

profile of v0, /device:TPU:1, one launch (start us, length us, event | category | flops | bytes accessed | tf_op | source)
XLA Modules:
  0.0 186.9 jit_solution(2766687566238518207)
XLA Ops:
  11.3 8.4 %all_gather.24 = bf16[1,6,37,1024]{3,2,0,1:T(8,128)(2,1)S(1)} all-gather(bf16[1,3,37,1024]{3,2,0,1:T(8,128)(2,1)S(1)} %multiply_convert_fusion.1), channel_id=1, replica_groups=mesh['scene'=2,'seq'=4,'head'=2,'band'=2] {'head'}, dimensions={1}, use_global_device_ids=true | all-gather | bytes 681984 | tf_op jit(solution)/shard_map/all_gather | solution.py:101
  19.8 1.7 fusion.34
  21.5 3.1 %all-gather.1 = bf16[2,222,512]{2,1,0:T(8,128)(2,1)S(1)} all-gather(bf16[1,222,512]{2,1,0:T(8,128)(2,1)S(1)} %fusion.34), channel_id=1, replica_groups=mesh['scene'=2,'seq'=4,'head'=2,'band'=2] {'band'}, dimensions={0}, use_global_device_ids=true | all-gather | bytes 681984 | tf_op jit(solution)/shard_map/all_gather | solution.py:125
  27.0 1.6 fusion.33
  28.7 2.1 %all-gather = bf16[2,222,512]{2,1,0:T(8,128)(2,1)S(1)} all-gather(bf16[1,222,512]{2,1,0:T(8,128)(2,1)S(1)} %fusion.33), channel_id=1, replica_groups=mesh['scene'=2,'seq'=4,'head'=2,'band'=2] {'band'}, dimensions={0}, use_global_device_ids=true | all-gather | bytes 681984 | tf_op jit(solution)/shard_map/all_gather | solution.py:126
  34.8 3.4 %all-to-all-start = ((bf16[2,111,512]{2,1,0:T(8,128)(2,1)}), bf16[2,111,512]{2,1,0:T(8,128)(2,1)S(1)}, u32[]{:S(2)}, u32[]{:S(2)}) async-start(bf16[2,111,512]{2,1,0:T(8,128)(2,1)} %copy.47), calls=%async_computation | async-start | bytes 458752 | tf_op jit(solution)/shard_map/all_to_all | solution.py:130
  38.5 7.6 %all-to-all-done = bf16[2,111,512]{2,1,0:T(8,128)(2,1)S(1)} async-done(((bf16[2,111,512]{2,1,0:T(8,128)(2,1)}), bf16[2,111,512]{2,1,0:T(8,128)(2,1)S(1)}, u32[]{:S(2)}, u32[]{:S(2)}) %all-to-all-start) | async-done | bytes 227360 | tf_op jit(solution)/shard_map/all_to_all | solution.py:130
  47.0 2.1 %convert_reduce_fusion.1 = (f32[111]{0:T(128)S(1)}, bf16[111,1024]{1,0:T(8,128)(2,1)S(1)}) fusion(f32[111,1024]{1,0:T(8,128)S(1)} %reshape.316, bf16[111,1024]{1,0:T(8,128)(2,1)S(1)} %bitcast.210, bf16[1024,1024]{1,0:T(8,128)(2,1)} %all-gather.9.cloned.1.call-done), kind=kOutput, calls=%fused_computation.81 | convolution fusion | flops 233238416 | bytes 3006908 | tf_op jit(solution)/shard_map/dot_general | solution.py:131
  49.8 7.3 %all_gather.28 = bf16[1,6,37,1024]{3,2,0,1:T(8,128)(2,1)S(1)} all-gather(bf16[1,3,37,1024]{3,2,0,1:T(8,128)(2,1)S(1)} %multiply_convert_fusion), channel_id=1, replica_groups=mesh['scene'=2,'seq'=4,'head'=2,'band'=2] {'head'}, dimensions={1}, use_global_device_ids=true | all-gather | bytes 681984 | tf_op jit(solution)/shard_map/all_gather | solution.py:101
  57.3 2.3 %fusion.35 = bf16[1,222,512]{2,1,0:T(8,128)(2,1)} fusion(bf16[222,1024]{1,0:T(8,128)(2,1)S(1)} %reshape.321, bf16[3,1024,512]{2,1,0:T(8,128)(2,1)} %param.18), kind=kOutput, calls=%fused_computation.41 | convolution fusion | flops 232897536 | bytes 1730560 | tf_op jit(solution)/shard_map/dot_general | solution.py:106
  59.7 2.3 %fusion.36 = bf16[1,222,512]{2,1,0:T(8,128)(2,1)} fusion(bf16[222,1024]{1,0:T(8,128)(2,1)S(1)} %reshape.321, bf16[3,1024,512]{2,1,0:T(8,128)(2,1)} %param.18), kind=kOutput, calls=%fused_computation.42 | convolution fusion | flops 232897536 | bytes 1730560 | tf_op jit(solution)/shard_map/dot_general | solution.py:109
  62.7 1.6 convolution_convert_fusion.1
  65.2 23.2 %all-gather.13.cloned.1.call-done = bf16[8,222,512]{2,1,0:T(8,128)(2,1)} async-done(((bf16[1,222,512]{2,1,0:T(8,128)(2,1)}), bf16[8,222,512]{2,1,0:T(8,128)(2,1)}) %all-gather.13.cloned.1.call-update) | async-done | bytes 1818640 | tf_op jit(solution)/shard_map/all_gather | solution.py:117
  88.3 2.7 %reshape.322 = bf16[2,888,512]{2,1,0:T(8,128)(2,1)} reshape(bf16[8,222,512]{2,1,0:T(8,128)(2,1)} %all-gather.13.cloned.1.call-done) | data formatting | bytes 3637248 | tf_op jit(solution)/shard_map/reshape | solution.py:75
  91.1 25.4 %all-gather.15.cloned.1.call-done = bf16[8,222,512]{2,1,0:T(8,128)(2,1)} async-done(((bf16[1,222,512]{2,1,0:T(8,128)(2,1)}), bf16[8,222,512]{2,1,0:T(8,128)(2,1)}) %all-gather.15.cloned.1.call-update) | async-done | bytes 1818640 | tf_op jit(solution)/shard_map/all_gather | solution.py:118
  116.4 2.6 %reshape.324 = bf16[2,888,512]{2,1,0:T(8,128)(2,1)} reshape(bf16[8,222,512]{2,1,0:T(8,128)(2,1)} %all-gather.15.cloned.1.call-done) | data formatting | bytes 3637248 | tf_op jit(solution)/shard_map/reshape | solution.py:76
  119.1 36.0 %while.15 = (s32[]{:T(128)}, f32[222,8]{0,1:T(8,128)S(1)}, f32[222,8]{0,1:T(8,128)S(1)}, f32[222,8,64]{0,2,1:T(8,128)S(1)}, bf16[2,888,512]{2,1,0:T(8,128)(2,1)}...) while((s32[]{:T(128)}, f32[222,8]{0,1:T(8,128)S(1)}, ...), condition=%wide.region_9.10_spmd.clone, body=%wide.region_6.9_spmd.clone.sunk | while | flops 416701120 | bytes 29268588 | solution.py:95
  119.1 2.5 %constant_dynamic-slice_fusion.3 = (bf16[1,888,512]{2,1,0:T(8,128)(2,1)S(1)}, bf16[1,888,512]{2,1,0:T(8,128)(2,1)}) fusion(bf16[2,888,512]{2,1,0:T(8,128)(2,1)} %get-tuple-element.201, s32[]{:T(128)} %get-tuple-element.186, bf16[2,888,512]{2,1,0:T(8,128)(2,1)} %get-tuple-element.199), kind=kLoop, calls=%fused_computation.15.clone.1 | loop fusion | bytes 3637252 | tf_op jit(solution)/shard_map/while/body/jit(dynamic_index_in_dim)/dynamic_slice | solution.py:95
  123.1 4.7 %bitcast_reduce_fusion.3 = (f32[222,8]{0,1:T(8,128)S(1)}, f32[8,888,222]{1,2,0:T(8,128)}) fusion(bf16[888,8,64]{0,2,1:T(8,128)(2,1)S(1)} %bitcast.207, bf16[222,8,64]{0,2,1:T(8,128)(2,1)} %get-tuple-element.200), kind=kOutput, calls=%fused_computation.1.clone.1 | convolution fusion | flops 205019664 | bytes 7452096 | tf_op jit(solution)/shard_map/while/body/eval_jaxpr/qhd,khd->qhk/dot_general | solution.py:80
  127.9 4.1 %fusion.127 = f32[222,8]{0,1:T(8,128)S(1)} fusion(f32[8,888,222]{1,2,0:T(8,128)} %get-tuple-element.173, f32[222,8]{0,1:T(8,128)S(1)} %select_maximum_fusion.2), kind=kLoop, calls=%fused_computation.4.clone.1 | loop fusion | flops 4729488 | bytes 6322560 | tf_op jit(solution)/shard_map/while/body/eval_jaxpr/reduce_sum | solution.py:86
  132.6 4.4 %fusion.129 = f32[222,8,64]{0,2,1:T(8,128)S(1)} fusion(bf16[888,8,64]{0,2,1:T(8,128)(2,1)S(1)} %bitcast.206, f32[8,888,222]{1,2,0:T(8,128)} %get-tuple-element.173, f32[222,8]{0,1:T(8,128)S(1)} %select_maximum_fusion.2, f32[222,8,64]{0,2,1:T(8,128)S(1)} %get-tuple-element.189, f32[222,8]{0,1:T(8,128)S(1)} %get-tuple-element.176, pred[]{:T(512)S(6)} %compare.44), kind=kOutput, calls=%fused_computation.9.clone.1 | convolution fusion | flops 206939520 | bytes 8141185 | tf_op jit(solution)/shard_map/while/body/eval_jaxpr/qhk,khd->qhd/dot_general | solution.py:87
  137.1 2.5 %constant_dynamic-slice_fusion.3 = (bf16[1,888,512]{2,1,0:T(8,128)(2,1)S(1)}, bf16[1,888,512]{2,1,0:T(8,128)(2,1)}) fusion(bf16[2,888,512]{2,1,0:T(8,128)(2,1)} %get-tuple-element.201, s32[]{:T(128)} %get-tuple-element.186, bf16[2,888,512]{2,1,0:T(8,128)(2,1)} %get-tuple-element.199), kind=kLoop, calls=%fused_computation.15.clone.1 | loop fusion | bytes 3637252 | tf_op jit(solution)/shard_map/while/body/jit(dynamic_index_in_dim)/dynamic_slice | solution.py:95
  141.1 4.7 %bitcast_reduce_fusion.3 = (f32[222,8]{0,1:T(8,128)S(1)}, f32[8,888,222]{1,2,0:T(8,128)}) fusion(bf16[888,8,64]{0,2,1:T(8,128)(2,1)S(1)} %bitcast.207, bf16[222,8,64]{0,2,1:T(8,128)(2,1)} %get-tuple-element.200), kind=kOutput, calls=%fused_computation.1.clone.1 | convolution fusion | flops 205019664 | bytes 7452096 | tf_op jit(solution)/shard_map/while/body/eval_jaxpr/qhd,khd->qhk/dot_general | solution.py:80
  145.8 4.1 %fusion.127 = f32[222,8]{0,1:T(8,128)S(1)} fusion(f32[8,888,222]{1,2,0:T(8,128)} %get-tuple-element.173, f32[222,8]{0,1:T(8,128)S(1)} %select_maximum_fusion.2), kind=kLoop, calls=%fused_computation.4.clone.1 | loop fusion | flops 4729488 | bytes 6322560 | tf_op jit(solution)/shard_map/while/body/eval_jaxpr/reduce_sum | solution.py:86
  150.6 4.4 %fusion.129 = f32[222,8,64]{0,2,1:T(8,128)S(1)} fusion(bf16[888,8,64]{0,2,1:T(8,128)(2,1)S(1)} %bitcast.206, f32[8,888,222]{1,2,0:T(8,128)} %get-tuple-element.173, f32[222,8]{0,1:T(8,128)S(1)} %select_maximum_fusion.2, f32[222,8,64]{0,2,1:T(8,128)S(1)} %get-tuple-element.189, f32[222,8]{0,1:T(8,128)S(1)} %get-tuple-element.176, pred[]{:T(512)S(6)} %compare.44), kind=kOutput, calls=%fused_computation.9.clone.1 | convolution fusion | flops 206939520 | bytes 8141185 | tf_op jit(solution)/shard_map/while/body/eval_jaxpr/qhk,khd->qhd/dot_general | solution.py:87
  156.2 3.6 %all-to-all-start.1 = ((bf16[2,111,512]{2,1,0:T(8,128)(2,1)}), bf16[2,111,512]{2,1,0:T(8,128)(2,1)S(1)}, u32[]{:S(2)}, u32[]{:S(2)}) async-start(bf16[2,111,512]{2,1,0:T(8,128)(2,1)} %copy.53), calls=%async_computation.1 | async-start | bytes 458752 | tf_op jit(solution)/shard_map/all_to_all | solution.py:130
  159.8 1.8 convert_element_type.136
  161.5 2.8 %all-to-all-done.1 = bf16[2,111,512]{2,1,0:T(8,128)(2,1)S(1)} async-done(((bf16[2,111,512]{2,1,0:T(8,128)(2,1)}), bf16[2,111,512]{2,1,0:T(8,128)(2,1)S(1)}, u32[]{:S(2)}, u32[]{:S(2)}) %all-to-all-start.1) | async-done | bytes 227360 | tf_op jit(solution)/shard_map/all_to_all | solution.py:130
  164.9 2.9 %fusion.97 = (f32[111,1024]{1,0:T(8,128)}, bf16[111,1024]{1,0:T(8,128)(2,1)S(1)}) fusion(bf16[111,1024]{1,0:T(8,128)(2,1)S(1)} %bitcast.211, bf16[1024,1024]{1,0:T(8,128)(2,1)} %all-gather.11.cloned.1.call-done, bf16[111,1024]{1,0:T(8,128)(2,1)S(1)} %copy-done.2), kind=kOutput, calls=%fused_computation.135 | convolution fusion | flops 233238528 | bytes 3233792 | tf_op jit(solution)/shard_map/dot_general | solution.py:131
  170.0 3.0 %collective-permute-start = (bf16[1,1,37,256]{3,2,1,0:T(8,128)(2,1)S(1)}, bf16[1,1,37,256]{3,2,1,0:T(8,128)(2,1)S(1)}, u32[]{:S(2)}, u32[]{:S(2)}) collective-permute-start(bf16[1,1,37,256]{3,2,1,0:T(8,128)(2,1)S(1)} %get-tuple-element.114), channel_id=1, source_target_pairs={{0,1},{1,2},{2,3},{4,5},{5,6},{6,7},{8,9},{9,10},{10,11},{12,13},{... | collective-permute-start | bytes 56840 | tf_op jit(solution)/shard_map/ppermute | solution.py:16
  173.0 1.9 %collective-permute-start.1 = (bf16[1,1,37,256]{3,2,1,0:T(8,128)(2,1)S(1)}, bf16[1,1,37,256]{3,2,1,0:T(8,128)(2,1)S(1)}, u32[]{:S(2)}, u32[]{:S(2)}) collective-permute-start(bf16[1,1,37,256]{3,2,1,0:T(8,128)(2,1)S(1)} %get-tuple-element.115), channel_id=1, source_target_pairs={{1,0},{2,1},{3,2},{5,4},{6,5},{7,6},{9,8},{10,9},{11,10},{13,12},{... | collective-permute-start | bytes 56840 | tf_op jit(solution)/shard_map/ppermute | solution.py:19
  175.0 3.1 %collective-permute-done.1 = bf16[1,1,37,256]{3,2,1,0:T(8,128)(2,1)S(1)} collective-permute-done((bf16[1,1,37,256]{3,2,1,0:T(8,128)(2,1)S(1)}, bf16[1,1,37,256]{3,2,1,0:T(8,128)(2,1)S(1)}, u32[]{:S(2)}, u32[]{:S(2)}) %collective-permute-start.1) | collective-permute-done | bytes 18976 | tf_op jit(solution)/shard_map/ppermute | solution.py:19
  (104 shorter events, 24.4 us)
Async XLA Ops:
  7.2 161.3 %copy-start = (bf16[2048,256]{1,0:T(8,128)(2,1)S(1)}, bf16[2048,256]{1,0:T(8,128)(2,1)}, u32[]{:S(2)}) copy-start(bf16[2048,256]{1,0:T(8,128)(2,1)} %param.21) | copy-start | bytes 3145732
  7.2 39.8 %all-gather.9.cloned.1.call-start = ((), (), s32[]{:S(2)}) async-start(), calls=%async_computation.2 | async-start | bytes 3145728 | tf_op jit(solution)/shard_map/all_gather | solution.py:133
  33.0 5.4 %copy-start.3 = (bf16[1,3,37,1024]{3,2,1,0:T(8,128)(2,1)S(1)}, bf16[1,3,37,1024]{3,2,1,0:T(8,128)(2,1)}, u32[]{:S(2)}) copy-start(bf16[1,3,37,1024]{3,2,1,0:T(8,128)(2,1)} %param.13) | copy-start | bytes 681988
  34.8 11.3 %all-to-all-start = ((bf16[2,111,512]{2,1,0:T(8,128)(2,1)}), bf16[2,111,512]{2,1,0:T(8,128)(2,1)S(1)}, u32[]{:S(2)}, u32[]{:S(2)}) async-start(bf16[2,111,512]{2,1,0:T(8,128)(2,1)} %copy.47), calls=%async_computation | async-start | bytes 458752 | tf_op jit(solution)/shard_map/all_to_all | solution.py:130
  38.3 50.1 %all-gather.13.cloned.1.call-start = ((), (), s32[]{:S(2)}) async-start(), calls=%async_computation.4 | async-start | bytes 2064384 | tf_op jit(solution)/shard_map/all_gather | solution.py:117
  38.4 11.3 %copy-start.8 = (f32[1024]{0:T(1024)S(1)}, f32[1024]{0:T(1024)}, u32[]{:S(2)}) copy-start(f32[1024]{0:T(1024)} %param.17) | copy-start | bytes 12292
  49.2 12.9 %copy-start.1 = (bf16[111,1024]{1,0:T(8,128)(2,1)}, bf16[111,1024]{1,0:T(8,128)(2,1)S(1)}, u32[]{:S(2)}) copy-start(bf16[111,1024]{1,0:T(8,128)(2,1)S(1)} %get-tuple-element.119) | copy-start | bytes 681988
  49.3 12.8 %copy-start.4 = (bf16[1,3,37,1024]{3,2,1,0:T(8,128)(2,1)}, bf16[1,3,37,1024]{3,2,1,0:T(8,128)(2,1)S(1)}, u32[]{:S(2)}) copy-start(bf16[1,3,37,1024]{3,2,1,0:T(8,128)(2,1)S(1)} %convert_element_type.137) | copy-start | bytes 681988
  59.7 56.8 %all-gather.15.cloned.1.call-start = ((), (), s32[]{:S(2)}) async-start(), calls=%async_computation.5 | async-start | bytes 2064384 | tf_op jit(solution)/shard_map/all_gather | solution.py:118
  62.1 102.7 %all-gather.11.cloned.1.call-start = ((), (), s32[]{:S(2)}) async-start(), calls=%async_computation.3 | async-start | bytes 3145728 | tf_op jit(solution)/shard_map/all_gather | solution.py:133
  155.0 9.8 %copy-start.2 = (bf16[111,1024]{1,0:T(8,128)(2,1)S(1)}, bf16[111,1024]{1,0:T(8,128)(2,1)}, u32[]{:S(2)}) copy-start(bf16[111,1024]{1,0:T(8,128)(2,1)} %copy-done.1) | copy-start | bytes 681988
  156.2 11.9 %copy-start.5 = (bf16[1,3,37,1024]{3,2,1,0:T(8,128)(2,1)S(1)}, bf16[1,3,37,1024]{3,2,1,0:T(8,128)(2,1)}, u32[]{:S(2)}) copy-start(bf16[1,3,37,1024]{3,2,1,0:T(8,128)(2,1)} %copy-done.4) | copy-start | bytes 681988
  156.2 8.2 %all-to-all-start.1 = ((bf16[2,111,512]{2,1,0:T(8,128)(2,1)}), bf16[2,111,512]{2,1,0:T(8,128)(2,1)S(1)}, u32[]{:S(2)}, u32[]{:S(2)}) async-start(bf16[2,111,512]{2,1,0:T(8,128)(2,1)} %copy.53), calls=%async_computation.1 | async-start | bytes 458752 | tf_op jit(solution)/shard_map/all_to_all | solution.py:130
  159.7 8.7 %copy-start.9 = (f32[2048]{0:T(1024)S(1)}, f32[2048]{0:T(1024)}, u32[]{:S(2)}) copy-start(f32[2048]{0:T(1024)} %param.20) | copy-start | bytes 24580
  159.8 8.7 %copy-start.10 = (f32[256]{0:T(256)S(1)}, f32[256]{0:T(256)}, u32[]{:S(2)}) copy-start(f32[256]{0:T(256)} %param.22) | copy-start | bytes 3076
  164.8 13.3 %copy-start.6 = (bf16[3,3,256,256]{3,2,1,0:T(8,128)(2,1)S(1)}, bf16[3,3,256,256]{3,2,1,0:T(8,128)(2,1)}, u32[]{:S(2)}) copy-start(bf16[3,3,256,256]{3,2,1,0:T(8,128)(2,1)} %param.23) | copy-start | bytes 3538948
  168.0 11.6 %copy-start.7 = (bf16[1,3,37,1024]{3,2,1,0:T(8,128)(2,1)}, bf16[1,3,37,1024]{3,2,1,0:T(8,128)(2,1)S(1)}, u32[]{:S(2)}) copy-start(bf16[1,3,37,1024]{3,2,1,0:T(8,128)(2,1)S(1)} %reshape.325) | copy-start | bytes 681988
  170.0 4.9 %collective-permute-start = (bf16[1,1,37,256]{3,2,1,0:T(8,128)(2,1)S(1)}, bf16[1,1,37,256]{3,2,1,0:T(8,128)(2,1)S(1)}, u32[]{:S(2)}, u32[]{:S(2)}) collective-permute-start(bf16[1,1,37,256]{3,2,1,0:T(8,128)(2,1)S(1)} %get-tuple-element.114), channel_id=1, source_target_pairs={{0,1},{1,2},{2,3},{4,5},{5,6},{6,7},{8,9},{9,10},{10,11},{12,13},{... | collective-permute-start | bytes 56840 | tf_op jit(solution)/shard_map/ppermute | solution.py:16
  173.0 5.1 %collective-permute-start.1 = (bf16[1,1,37,256]{3,2,1,0:T(8,128)(2,1)S(1)}, bf16[1,1,37,256]{3,2,1,0:T(8,128)(2,1)S(1)}, u32[]{:S(2)}, u32[]{:S(2)}) collective-permute-start(bf16[1,1,37,256]{3,2,1,0:T(8,128)(2,1)S(1)} %get-tuple-element.115), channel_id=1, source_target_pairs={{1,0},{2,1},{3,2},{5,4},{6,5},{7,6},{9,8},{10,9},{11,10},{13,12},{... | collective-permute-start | bytes 56840 | tf_op jit(solution)/shard_map/ppermute | solution.py:19
Sparse Core Ops, SparseCore 0:
  9.5 37.4 all-gather.8
  59.8 28.5 all-gather.12
  90.0 26.3 all-gather.14
  117.8 31.9 all-gather.10
where the time goes:
time: 188 us; the launch traced here: 187 us
  waiting for transfers between devices  63.7 us (34%)
  matrix products  39.8 us (21%)
  local copies, waits for them, and re-layouts  21 us (11%)
  blocking collectives  20.9 us (11%)
  other arithmetic  15 us (8%)
  between operations  14.2 us (8%)
  starting transfers between devices  12.2 us (6%)
    all_gather x1, waiting for transfers between devices, attention_block(): lax.all_gather(value_rows, ('seq', 'band'), axis=0, tiled=True)  25.4 us
    all_gather x1, waiting for transfers between devices, attention_block(): lax.all_gather(key_rows, ('seq', 'band'), axis=0, tiled=True)  23.2 us
    all_gather x2, blocking collectives, attention_block(): gathered = lax.all_gather(normed, 'head', axis=1, tiled=True)  15.7 us
    all_to_all x2, waiting for transfers between devices, attention_block(): lax.all_to_all(attended, 'head', split_axis=0, concat_axis=1, tiled=True)  10.5 us
    dot_general x2, matrix products, absorb(): jnp.einsum('qhd,khd->qhk', heads_q, by_heads(blocks_pair[0]), preferred_e...  9.42 us
    dynamic_slice x6, local copies, waits for them, and re-layouts, fold_keys(): carry, ignored = lax.scan(absorb, carry, (key_blocks, value_blocks))  9.3 us
    dot_general x2, matrix products, absorb(): jnp.einsum('qhk,khd->qhd', probs.astype(jnp.bfloat16), by_heads(blocks_pa...  8.89 us
    reduce_sum x2, other arithmetic, absorb(): running_sum = running_sum * decay + jnp.sum(probs, axis=-1)  8.21 us
  transfers between devices with their start and end apart: 8, of which 6 were waited for; matrix products, arithmetic and copies ran while one was open for 34% of the time, Pallas kernels for 0%

commit v1 on v0

--- a/solution.py
+++ b/solution.py
@@ -127,7 +127,10 @@
         )
         attended = attend_local(query_rows, keys_all, values_all)
     band_rows = inputs.shape[1] * inputs.shape[2]
-    own_rows = lax.all_to_all(attended, "head", split_axis=0, concat_axis=1, tiled=True)
+    own_rows = jnp.concatenate(
+        lax.all_to_all(jnp.stack(jnp.split(attended, lax.axis_size("head"), axis=0)), "head", 0, 0),
+        axis=1,
+    )
     branch = jnp.dot(
         own_rows,
         lax.all_gather(out_weight, "head", axis=0, tiled=True),

time: 188 us -> 188 us (level)
    convert_element_type x4 -> x0, local copies, waits for them, and re-layouts: 2.11 us -> none  [the longest x2 1.06 us: attend_local(): return mixed.reshape(queries.shape).astype(jnp.bfloat16)]
where the time goes in v1:
time: 188 us; the launch traced here: 187 us
  waiting for transfers between devices  63.7 us (34%)
  matrix products  39.8 us (21%)
  blocking collectives  20.9 us (11%)
  local copies, waits for them, and re-layouts  20.2 us (11%)
  other arithmetic  15.8 us (8%)
  between operations  14.2 us (8%)
  starting transfers between devices  12.2 us (6%)
    all_gather x1, waiting for transfers between devices, attention_block(): lax.all_gather(value_rows, ('seq', 'band'), axis=0, tiled=True)  25.4 us
    all_gather x1, waiting for transfers between devices, attention_block(): lax.all_gather(key_rows, ('seq', 'band'), axis=0, tiled=True)  23.2 us
    all_gather x2, blocking collectives, attention_block(): gathered = lax.all_gather(normed, 'head', axis=1, tiled=True)  15.7 us
    all_to_all x2, waiting for transfers between devices, attention_block(): lax.all_to_all(jnp.stack(jnp.split(attended, lax.axis_size('head'), axis=...  10.5 us
    dot_general x2, matrix products, absorb(): jnp.einsum('qhd,khd->qhk', heads_q, by_heads(blocks_pair[0]), preferred_e...  9.44 us
    dynamic_slice x6, local copies, waits for them, and re-layouts, fold_keys(): carry, ignored = lax.scan(absorb, carry, (key_blocks, value_blocks))  9.28 us
    dot_general x2, matrix products, absorb(): jnp.einsum('qhk,khd->qhd', probs.astype(jnp.bfloat16), by_heads(blocks_pa...  8.89 us
    reduce_sum x2, other arithmetic, absorb(): running_sum = running_sum * decay + jnp.sum(probs, axis=-1)  8.21 us
  transfers between devices with their start and end apart: 8, of which 6 were waited for; matrix products, arithmetic and copies ran while one was open for 34% of the time, Pallas kernels for 0%

profile of v1, /device:TPU:1, one launch (start us, length us, event | category | flops | bytes accessed | tf_op | source)
XLA Modules:
  0.0 186.9 jit_solution(16472195319417803567)
XLA Ops:
  11.3 8.4 %all_gather.24 = bf16[1,6,37,1024]{3,2,0,1:T(8,128)(2,1)S(1)} all-gather(bf16[1,3,37,1024]{3,2,0,1:T(8,128)(2,1)S(1)} %multiply_convert_fusion.1), channel_id=1, replica_groups=mesh['scene'=2,'seq'=4,'head'=2,'band'=2] {'head'}, dimensions={1}, use_global_device_ids=true | all-gather | bytes 681984 | tf_op jit(solution)/shard_map/all_gather | solution.py:101
  19.8 1.7 fusion.34
  21.5 3.1 %all-gather.1 = bf16[2,222,512]{2,1,0:T(8,128)(2,1)S(1)} all-gather(bf16[1,222,512]{2,1,0:T(8,128)(2,1)S(1)} %fusion.34), channel_id=1, replica_groups=mesh['scene'=2,'seq'=4,'head'=2,'band'=2] {'band'}, dimensions={0}, use_global_device_ids=true | all-gather | bytes 681984 | tf_op jit(solution)/shard_map/all_gather | solution.py:125
  27.0 1.6 fusion.33
  28.7 2.1 %all-gather = bf16[2,222,512]{2,1,0:T(8,128)(2,1)S(1)} all-gather(bf16[1,222,512]{2,1,0:T(8,128)(2,1)S(1)} %fusion.33), channel_id=1, replica_groups=mesh['scene'=2,'seq'=4,'head'=2,'band'=2] {'band'}, dimensions={0}, use_global_device_ids=true | all-gather | bytes 681984 | tf_op jit(solution)/shard_map/all_gather | solution.py:126
  34.9 3.4 %all-to-all-start = ((bf16[2,111,512]{2,1,0:T(8,128)(2,1)}), bf16[2,111,512]{2,1,0:T(8,128)(2,1)S(1)}, u32[]{:S(2)}, u32[]{:S(2)}) async-start(bf16[2,111,512]{2,1,0:T(8,128)(2,1)} %pad_maximum_fusion.1), calls=%async_computation | async-start | bytes 458752 | tf_op jit(solution)/shard_map/all_to_all | solution.py:131
  38.5 7.6 %all-to-all-done = bf16[2,111,512]{2,1,0:T(8,128)(2,1)S(1)} async-done(((bf16[2,111,512]{2,1,0:T(8,128)(2,1)}), bf16[2,111,512]{2,1,0:T(8,128)(2,1)S(1)}, u32[]{:S(2)}, u32[]{:S(2)}) %all-to-all-start) | async-done | bytes 227360 | tf_op jit(solution)/shard_map/all_to_all | solution.py:131
  47.0 2.1 %convert_reduce_fusion.1 = (f32[111]{0:T(128)S(1)}, bf16[111,1024]{1,0:T(8,128)(2,1)S(1)}) fusion(f32[111,1024]{1,0:T(8,128)S(1)} %reshape.328, bf16[111,1024]{1,0:T(8,128)(2,1)S(1)} %bitcast.210, bf16[1024,1024]{1,0:T(8,128)(2,1)} %all-gather.9.cloned.1.call-done), kind=kOutput, calls=%fused_computation.81 | convolution fusion | flops 233238416 | bytes 3006908 | tf_op jit(solution)/shard_map/dot_general | solution.py:134
  49.8 7.3 %all_gather.28 = bf16[1,6,37,1024]{3,2,0,1:T(8,128)(2,1)S(1)} all-gather(bf16[1,3,37,1024]{3,2,0,1:T(8,128)(2,1)S(1)} %multiply_convert_fusion), channel_id=1, replica_groups=mesh['scene'=2,'seq'=4,'head'=2,'band'=2] {'head'}, dimensions={1}, use_global_device_ids=true | all-gather | bytes 681984 | tf_op jit(solution)/shard_map/all_gather | solution.py:101
  57.3 2.3 %fusion.35 = bf16[1,222,512]{2,1,0:T(8,128)(2,1)} fusion(bf16[222,1024]{1,0:T(8,128)(2,1)S(1)} %reshape.335, bf16[3,1024,512]{2,1,0:T(8,128)(2,1)} %param.18), kind=kOutput, calls=%fused_computation.41 | convolution fusion | flops 232897536 | bytes 1730560 | tf_op jit(solution)/shard_map/dot_general | solution.py:106
  59.7 2.3 %fusion.36 = bf16[1,222,512]{2,1,0:T(8,128)(2,1)} fusion(bf16[222,1024]{1,0:T(8,128)(2,1)S(1)} %reshape.335, bf16[3,1024,512]{2,1,0:T(8,128)(2,1)} %param.18), kind=kOutput, calls=%fused_computation.42 | convolution fusion | flops 232897536 | bytes 1730560 | tf_op jit(solution)/shard_map/dot_general | solution.py:109
  62.7 1.6 convolution_convert_fusion.1
  65.2 23.2 %all-gather.13.cloned.1.call-done = bf16[8,222,512]{2,1,0:T(8,128)(2,1)} async-done(((bf16[1,222,512]{2,1,0:T(8,128)(2,1)}), bf16[8,222,512]{2,1,0:T(8,128)(2,1)}) %all-gather.13.cloned.1.call-update) | async-done | bytes 1818640 | tf_op jit(solution)/shard_map/all_gather | solution.py:117
  88.4 2.7 %reshape.336 = bf16[2,888,512]{2,1,0:T(8,128)(2,1)} reshape(bf16[8,222,512]{2,1,0:T(8,128)(2,1)} %all-gather.13.cloned.1.call-done) | data formatting | bytes 3637248 | tf_op jit(solution)/shard_map/reshape | solution.py:75
  91.1 25.4 %all-gather.15.cloned.1.call-done = bf16[8,222,512]{2,1,0:T(8,128)(2,1)} async-done(((bf16[1,222,512]{2,1,0:T(8,128)(2,1)}), bf16[8,222,512]{2,1,0:T(8,128)(2,1)}) %all-gather.15.cloned.1.call-update) | async-done | bytes 1818640 | tf_op jit(solution)/shard_map/all_gather | solution.py:118
  116.5 2.6 %reshape.338 = bf16[2,888,512]{2,1,0:T(8,128)(2,1)} reshape(bf16[8,222,512]{2,1,0:T(8,128)(2,1)} %all-gather.15.cloned.1.call-done) | data formatting | bytes 3637248 | tf_op jit(solution)/shard_map/reshape | solution.py:76
  119.1 36.0 %while.15 = (s32[]{:T(128)}, f32[222,8]{0,1:T(8,128)S(1)}, f32[222,8]{0,1:T(8,128)S(1)}, f32[222,8,64]{0,2,1:T(8,128)S(1)}, bf16[2,888,512]{2,1,0:T(8,128)(2,1)}...) while((s32[]{:T(128)}, f32[222,8]{0,1:T(8,128)S(1)}, ...), condition=%wide.region_9.10_spmd.clone, body=%wide.region_6.9_spmd.clone.sunk | while | flops 416701120 | bytes 29268588 | solution.py:95
  119.1 2.5 %constant_dynamic-slice_fusion.3 = (bf16[1,888,512]{2,1,0:T(8,128)(2,1)S(1)}, bf16[1,888,512]{2,1,0:T(8,128)(2,1)}) fusion(bf16[2,888,512]{2,1,0:T(8,128)(2,1)} %get-tuple-element.205, s32[]{:T(128)} %get-tuple-element.190, bf16[2,888,512]{2,1,0:T(8,128)(2,1)} %get-tuple-element.203), kind=kLoop, calls=%fused_computation.15.clone.1 | loop fusion | bytes 3637252 | tf_op jit(solution)/shard_map/while/body/jit(dynamic_index_in_dim)/dynamic_slice | solution.py:95
  123.2 4.7 %bitcast_reduce_fusion.3 = (f32[222,8]{0,1:T(8,128)S(1)}, f32[8,888,222]{1,2,0:T(8,128)}) fusion(bf16[888,8,64]{0,2,1:T(8,128)(2,1)S(1)} %bitcast.207, bf16[222,8,64]{0,2,1:T(8,128)(2,1)} %get-tuple-element.204), kind=kOutput, calls=%fused_computation.1.clone.1 | convolution fusion | flops 205019664 | bytes 7452096 | tf_op jit(solution)/shard_map/while/body/eval_jaxpr/qhd,khd->qhk/dot_general | solution.py:80
  127.9 4.1 %fusion.129 = f32[222,8]{0,1:T(8,128)S(1)} fusion(f32[8,888,222]{1,2,0:T(8,128)} %get-tuple-element.177, f32[222,8]{0,1:T(8,128)S(1)} %select_maximum_fusion.2), kind=kLoop, calls=%fused_computation.4.clone.1 | loop fusion | flops 4729488 | bytes 6322560 | tf_op jit(solution)/shard_map/while/body/eval_jaxpr/reduce_sum | solution.py:86
  132.6 4.4 %fusion.131 = f32[222,8,64]{0,2,1:T(8,128)S(1)} fusion(bf16[888,8,64]{0,2,1:T(8,128)(2,1)S(1)} %bitcast.206, f32[8,888,222]{1,2,0:T(8,128)} %get-tuple-element.177, f32[222,8]{0,1:T(8,128)S(1)} %select_maximum_fusion.2, f32[222,8,64]{0,2,1:T(8,128)S(1)} %get-tuple-element.193, f32[222,8]{0,1:T(8,128)S(1)} %get-tuple-element.180, pred[]{:T(512)S(6)} %compare.44), kind=kOutput, calls=%fused_computation.9.clone.1 | convolution fusion | flops 206939520 | bytes 8141185 | tf_op jit(solution)/shard_map/while/body/eval_jaxpr/qhk,khd->qhd/dot_general | solution.py:87
  137.1 2.5 %constant_dynamic-slice_fusion.3 = (bf16[1,888,512]{2,1,0:T(8,128)(2,1)S(1)}, bf16[1,888,512]{2,1,0:T(8,128)(2,1)}) fusion(bf16[2,888,512]{2,1,0:T(8,128)(2,1)} %get-tuple-element.205, s32[]{:T(128)} %get-tuple-element.190, bf16[2,888,512]{2,1,0:T(8,128)(2,1)} %get-tuple-element.203), kind=kLoop, calls=%fused_computation.15.clone.1 | loop fusion | bytes 3637252 | tf_op jit(solution)/shard_map/while/body/jit(dynamic_index_in_dim)/dynamic_slice | solution.py:95
  141.1 4.7 %bitcast_reduce_fusion.3 = (f32[222,8]{0,1:T(8,128)S(1)}, f32[8,888,222]{1,2,0:T(8,128)}) fusion(bf16[888,8,64]{0,2,1:T(8,128)(2,1)S(1)} %bitcast.207, bf16[222,8,64]{0,2,1:T(8,128)(2,1)} %get-tuple-element.204), kind=kOutput, calls=%fused_computation.1.clone.1 | convolution fusion | flops 205019664 | bytes 7452096 | tf_op jit(solution)/shard_map/while/body/eval_jaxpr/qhd,khd->qhk/dot_general | solution.py:80
  145.9 4.1 %fusion.129 = f32[222,8]{0,1:T(8,128)S(1)} fusion(f32[8,888,222]{1,2,0:T(8,128)} %get-tuple-element.177, f32[222,8]{0,1:T(8,128)S(1)} %select_maximum_fusion.2), kind=kLoop, calls=%fused_computation.4.clone.1 | loop fusion | flops 4729488 | bytes 6322560 | tf_op jit(solution)/shard_map/while/body/eval_jaxpr/reduce_sum | solution.py:86
  150.6 4.4 %fusion.131 = f32[222,8,64]{0,2,1:T(8,128)S(1)} fusion(bf16[888,8,64]{0,2,1:T(8,128)(2,1)S(1)} %bitcast.206, f32[8,888,222]{1,2,0:T(8,128)} %get-tuple-element.177, f32[222,8]{0,1:T(8,128)S(1)} %select_maximum_fusion.2, f32[222,8,64]{0,2,1:T(8,128)S(1)} %get-tuple-element.193, f32[222,8]{0,1:T(8,128)S(1)} %get-tuple-element.180, pred[]{:T(512)S(6)} %compare.44), kind=kOutput, calls=%fused_computation.9.clone.1 | convolution fusion | flops 206939520 | bytes 8141185 | tf_op jit(solution)/shard_map/while/body/eval_jaxpr/qhk,khd->qhd/dot_general | solution.py:87
  156.2 3.6 %all-to-all-start.1 = ((bf16[2,111,512]{2,1,0:T(8,128)(2,1)}), bf16[2,111,512]{2,1,0:T(8,128)(2,1)S(1)}, u32[]{:S(2)}, u32[]{:S(2)}) async-start(bf16[2,111,512]{2,1,0:T(8,128)(2,1)} %copy.52), calls=%async_computation.1 | async-start | bytes 458752 | tf_op jit(solution)/shard_map/all_to_all | solution.py:131
  159.8 1.8 convert_element_type.129
  161.5 2.8 %all-to-all-done.1 = bf16[2,111,512]{2,1,0:T(8,128)(2,1)S(1)} async-done(((bf16[2,111,512]{2,1,0:T(8,128)(2,1)}), bf16[2,111,512]{2,1,0:T(8,128)(2,1)S(1)}, u32[]{:S(2)}, u32[]{:S(2)}) %all-to-all-start.1) | async-done | bytes 227360 | tf_op jit(solution)/shard_map/all_to_all | solution.py:131
  164.9 2.9 %fusion.99 = (f32[111,1024]{1,0:T(8,128)}, bf16[111,1024]{1,0:T(8,128)(2,1)S(1)}) fusion(bf16[111,1024]{1,0:T(8,128)(2,1)S(1)} %bitcast.211, bf16[1024,1024]{1,0:T(8,128)(2,1)} %all-gather.11.cloned.1.call-done, bf16[111,1024]{1,0:T(8,128)(2,1)S(1)} %copy-done.2), kind=kOutput, calls=%fused_computation.139 | convolution fusion | flops 233238528 | bytes 3233792 | tf_op jit(solution)/shard_map/dot_general | solution.py:134
  170.0 2.9 %collective-permute-start = (bf16[1,1,37,256]{3,2,1,0:T(8,128)(2,1)S(1)}, bf16[1,1,37,256]{3,2,1,0:T(8,128)(2,1)S(1)}, u32[]{:S(2)}, u32[]{:S(2)}) collective-permute-start(bf16[1,1,37,256]{3,2,1,0:T(8,128)(2,1)S(1)} %get-tuple-element.118), channel_id=1, source_target_pairs={{0,1},{1,2},{2,3},{4,5},{5,6},{6,7},{8,9},{9,10},{10,11},{12,13},{... | collective-permute-start | bytes 56840 | tf_op jit(solution)/shard_map/ppermute | solution.py:16
  173.0 1.9 %collective-permute-start.1 = (bf16[1,1,37,256]{3,2,1,0:T(8,128)(2,1)S(1)}, bf16[1,1,37,256]{3,2,1,0:T(8,128)(2,1)S(1)}, u32[]{:S(2)}, u32[]{:S(2)}) collective-permute-start(bf16[1,1,37,256]{3,2,1,0:T(8,128)(2,1)S(1)} %get-tuple-element.119), channel_id=1, source_target_pairs={{1,0},{2,1},{3,2},{5,4},{6,5},{7,6},{9,8},{10,9},{11,10},{13,12},{... | collective-permute-start | bytes 56840 | tf_op jit(solution)/shard_map/ppermute | solution.py:19
  175.0 3.1 %collective-permute-done.1 = bf16[1,1,37,256]{3,2,1,0:T(8,128)(2,1)S(1)} collective-permute-done((bf16[1,1,37,256]{3,2,1,0:T(8,128)(2,1)S(1)}, bf16[1,1,37,256]{3,2,1,0:T(8,128)(2,1)S(1)}, u32[]{:S(2)}, u32[]{:S(2)}) %collective-permute-start.1) | collective-permute-done | bytes 18976 | tf_op jit(solution)/shard_map/ppermute | solution.py:19
  (107 shorter events, 24.4 us)
Async XLA Ops:
  7.2 161.3 %copy-start = (bf16[2048,256]{1,0:T(8,128)(2,1)S(1)}, bf16[2048,256]{1,0:T(8,128)(2,1)}, u32[]{:S(2)}) copy-start(bf16[2048,256]{1,0:T(8,128)(2,1)} %param.21) | copy-start | bytes 3145732
  7.2 39.8 %all-gather.9.cloned.1.call-start = ((), (), s32[]{:S(2)}) async-start(), calls=%async_computation.2 | async-start | bytes 3145728 | tf_op jit(solution)/shard_map/all_gather | solution.py:136
  33.0 5.4 %copy-start.3 = (bf16[1,3,37,1024]{3,2,1,0:T(8,128)(2,1)S(1)}, bf16[1,3,37,1024]{3,2,1,0:T(8,128)(2,1)}, u32[]{:S(2)}) copy-start(bf16[1,3,37,1024]{3,2,1,0:T(8,128)(2,1)} %param.13) | copy-start | bytes 681988
  34.9 11.3 %all-to-all-start = ((bf16[2,111,512]{2,1,0:T(8,128)(2,1)}), bf16[2,111,512]{2,1,0:T(8,128)(2,1)S(1)}, u32[]{:S(2)}, u32[]{:S(2)}) async-start(bf16[2,111,512]{2,1,0:T(8,128)(2,1)} %pad_maximum_fusion.1), calls=%async_computation | async-start | bytes 458752 | tf_op jit(solution)/shard_map/all_to_all | solution.py:131
  38.3 50.1 %all-gather.13.cloned.1.call-start = ((), (), s32[]{:S(2)}) async-start(), calls=%async_computation.4 | async-start | bytes 2064384 | tf_op jit(solution)/shard_map/all_gather | solution.py:117
  38.4 11.2 %copy-start.8 = (f32[1024]{0:T(1024)S(1)}, f32[1024]{0:T(1024)}, u32[]{:S(2)}) copy-start(f32[1024]{0:T(1024)} %param.17) | copy-start | bytes 12292
  49.2 12.9 %copy-start.1 = (bf16[111,1024]{1,0:T(8,128)(2,1)}, bf16[111,1024]{1,0:T(8,128)(2,1)S(1)}, u32[]{:S(2)}) copy-start(bf16[111,1024]{1,0:T(8,128)(2,1)S(1)} %get-tuple-element.123) | copy-start | bytes 681988
  49.3 12.8 %copy-start.4 = (bf16[1,3,37,1024]{3,2,1,0:T(8,128)(2,1)}, bf16[1,3,37,1024]{3,2,1,0:T(8,128)(2,1)S(1)}, u32[]{:S(2)}) copy-start(bf16[1,3,37,1024]{3,2,1,0:T(8,128)(2,1)S(1)} %convert_element_type.130) | copy-start | bytes 681988
  59.7 56.8 %all-gather.15.cloned.1.call-start = ((), (), s32[]{:S(2)}) async-start(), calls=%async_computation.5 | async-start | bytes 2064384 | tf_op jit(solution)/shard_map/all_gather | solution.py:118
  62.1 102.8 %all-gather.11.cloned.1.call-start = ((), (), s32[]{:S(2)}) async-start(), calls=%async_computation.3 | async-start | bytes 3145728 | tf_op jit(solution)/shard_map/all_gather | solution.py:136
  155.1 9.8 %copy-start.2 = (bf16[111,1024]{1,0:T(8,128)(2,1)S(1)}, bf16[111,1024]{1,0:T(8,128)(2,1)}, u32[]{:S(2)}) copy-start(bf16[111,1024]{1,0:T(8,128)(2,1)} %copy-done.1) | copy-start | bytes 681988
  156.2 11.9 %copy-start.5 = (bf16[1,3,37,1024]{3,2,1,0:T(8,128)(2,1)S(1)}, bf16[1,3,37,1024]{3,2,1,0:T(8,128)(2,1)}, u32[]{:S(2)}) copy-start(bf16[1,3,37,1024]{3,2,1,0:T(8,128)(2,1)} %copy-done.4) | copy-start | bytes 681988
  156.2 8.2 %all-to-all-start.1 = ((bf16[2,111,512]{2,1,0:T(8,128)(2,1)}), bf16[2,111,512]{2,1,0:T(8,128)(2,1)S(1)}, u32[]{:S(2)}, u32[]{:S(2)}) async-start(bf16[2,111,512]{2,1,0:T(8,128)(2,1)} %copy.52), calls=%async_computation.1 | async-start | bytes 458752 | tf_op jit(solution)/shard_map/all_to_all | solution.py:131
  159.8 8.7 %copy-start.9 = (f32[2048]{0:T(1024)S(1)}, f32[2048]{0:T(1024)}, u32[]{:S(2)}) copy-start(f32[2048]{0:T(1024)} %param.20) | copy-start | bytes 24580
  159.8 8.7 %copy-start.10 = (f32[256]{0:T(256)S(1)}, f32[256]{0:T(256)}, u32[]{:S(2)}) copy-start(f32[256]{0:T(256)} %param.22) | copy-start | bytes 3076
  164.9 13.3 %copy-start.6 = (bf16[3,3,256,256]{3,2,1,0:T(8,128)(2,1)S(1)}, bf16[3,3,256,256]{3,2,1,0:T(8,128)(2,1)}, u32[]{:S(2)}) copy-start(bf16[3,3,256,256]{3,2,1,0:T(8,128)(2,1)} %param.23) | copy-start | bytes 3538948
  168.0 11.6 %copy-start.7 = (bf16[1,3,37,1024]{3,2,1,0:T(8,128)(2,1)}, bf16[1,3,37,1024]{3,2,1,0:T(8,128)(2,1)S(1)}, u32[]{:S(2)}) copy-start(bf16[1,3,37,1024]{3,2,1,0:T(8,128)(2,1)S(1)} %reshape.341) | copy-start | bytes 681988
  170.0 4.9 %collective-permute-start = (bf16[1,1,37,256]{3,2,1,0:T(8,128)(2,1)S(1)}, bf16[1,1,37,256]{3,2,1,0:T(8,128)(2,1)S(1)}, u32[]{:S(2)}, u32[]{:S(2)}) collective-permute-start(bf16[1,1,37,256]{3,2,1,0:T(8,128)(2,1)S(1)} %get-tuple-element.118), channel_id=1, source_target_pairs={{0,1},{1,2},{2,3},{4,5},{5,6},{6,7},{8,9},{9,10},{10,11},{12,13},{... | collective-permute-start | bytes 56840 | tf_op jit(solution)/shard_map/ppermute | solution.py:16
  173.0 5.1 %collective-permute-start.1 = (bf16[1,1,37,256]{3,2,1,0:T(8,128)(2,1)S(1)}, bf16[1,1,37,256]{3,2,1,0:T(8,128)(2,1)S(1)}, u32[]{:S(2)}, u32[]{:S(2)}) collective-permute-start(bf16[1,1,37,256]{3,2,1,0:T(8,128)(2,1)S(1)} %get-tuple-element.119), channel_id=1, source_target_pairs={{1,0},{2,1},{3,2},{5,4},{6,5},{7,6},{9,8},{10,9},{11,10},{13,12},{... | collective-permute-start | bytes 56840 | tf_op jit(solution)/shard_map/ppermute | solution.py:19
Sparse Core Ops, SparseCore 0:
  9.5 37.4 all-gather.8
  59.8 28.5 all-gather.12
  90.0 26.3 all-gather.14
  117.9 31.9 all-gather.10
